TPU v7x, 32 devices: a whole 2x2x4 slice. The times are simulated.
32 devices in a mesh: grp: 4 (over y, x), tile: 8 (over z, core).
Axes of the slice: x: 2, y: 2, z: 4, core: 2. Of those that a mesh axis runs over, the one named last changes fastest.
Arguments:
- observed: bfloat16 [512, 32, 2048], P('tile', 'grp'), as said below
- visible: int32 [32, 2048], P('grp', 'tile'), may hold values from 0 to 65535
- params_start: float32 [8, 32, 2048], P(None, 'grp', 'tile'), may hold values from -1.5 to 1.5, as said below
- light_directions: float32 [3, 32], replicated, may hold values from -1 to 1
- view_dirs: float32 [3, 16], replicated, may hold values from -1 to 1
- gains_start: float32 [32], replicated, may hold values from 0.5 to 1.5
Outputs:
- params_out: float32 [8, 32, 2048], P(None, 'grp', 'tile')
- gains_out: float32 [32], replicated
Inputs may be any that keep to these rules, and one draw needn't show every extreme that they name: `observed`: luminance is positive. `params_start`: tilts within -0.3 to 0.3, diffuse 0.3 to 1.2, specular 0.1 to 0.8, sharpness logit -1.5 to 1.5, ambient -0.2 to 0.3, rim 0 to 0.5, retro -0.3 to 0.3.
All inputs are finite; a program needn't handle non-finite values.
Results may differ from a plain program's by a relative error of at most 0.0003.
Values may be sent and summed in bfloat16 or wider, within the bound.
No kernel may reach another device: no remote copies, remote signals or barrier semaphores. Data moves between devices by JAX's collectives and lax.ppermute only.
A program may use at most 64 MiB of HBM per device.

v0:
```python
import jax
import jax.numpy as jnp
from jax import lax
from jax.sharding import PartitionSpec as P

CAMS = 16
LIGHTS = 32
ITERS = 2
damping = 4.0
lift_z = 1.6


def padded_2(cells, sides, width):
    for axis, dim in sides:
        count = lax.axis_size(axis)
        ends = count - 1
        head = lax.slice_in_dim(cells, 0, width, axis=dim)
        tail = lax.slice_in_dim(cells, cells.shape[dim] - width, cells.shape[dim], axis=dim)
        cells = jnp.concatenate(
            [
                lax.ppermute(tail, axis, [(i, (i + 1) % count) for i in range(ends)]),
                cells,
                lax.ppermute(head, axis, [((i + 1) % count, i) for i in range(ends)]),
            ],
            axis=dim,
        )
    return cells


def unit_columns(raw):
    lifted = raw + jnp.array([0.0, 0.0, lift_z], jnp.float32)[:, None]
    return lifted / jnp.sqrt(jnp.sum(lifted * lifted, axis=0, keepdims=True))


def geometry(light_directions, view_dirs):
    lights = unit_columns(light_directions)
    views = unit_columns(view_dirs)
    raw_half = views.T[:, :, None] + lights[None]
    halves = raw_half / jnp.sqrt(jnp.sum(raw_half * raw_half, axis=1, keepdims=True))
    echoes = jnp.sum(views.T[:, :, None] * lights[None], axis=1)
    return (lights, halves, views.T, echoes)


def facing(dir_x, dir_y, dir_z, tilt_u, tilt_v, scale_q):
    facing_dot = (dir_x * tilt_u + dir_y * tilt_v + dir_z) * scale_q
    by_u = (dir_x - facing_dot * tilt_u * scale_q) * scale_q
    by_v = (dir_y - facing_dot * tilt_v * scale_q) * scale_q
    return (facing_dot, by_u, by_v)


def camera_terms(observed_c, weight_c, params, gains, lights, half_c, view_c, echo_c):
    tilt_u, tilt_v, diffuse, specular, sharp_raw, ambient, rim_gain, retro_gain = [
        params[i] for i in range(8)
    ]
    scale_q = 1.0 / jnp.sqrt(1.0 + tilt_u * tilt_u + tilt_v * tilt_v)
    light_dot, light_u, light_v = facing(
        lights[0][:, None], lights[1][:, None], lights[2][:, None], tilt_u, tilt_v, scale_q
    )
    half_dot, half_u, half_v = facing(
        half_c[0][:, None], half_c[1][:, None], half_c[2][:, None], tilt_u, tilt_v, scale_q
    )
    view_dot, view_u, view_v = facing(view_c[0], view_c[1], view_c[2], tilt_u, tilt_v, scale_q)
    sigma = jax.nn.sigmoid(sharp_raw)
    sharp = 1.0 + 20.0 * sigma
    lobe = jnp.exp(sharp * (half_dot - 1.0))
    back = 1.0 - view_dot
    rim_shape = back * back
    shaped = (
        diffuse * light_dot
        + specular * lobe
        + ambient
        + rim_gain * rim_shape
        + retro_gain * echo_c[:, None]
    )
    full = light_dot.shape
    jacob = [
        diffuse * light_u + specular * sharp * lobe * half_u - 2.0 * rim_gain * back * view_u,
        diffuse * light_v + specular * sharp * lobe * half_v - 2.0 * rim_gain * back * view_v,
        light_dot,
        lobe,
        specular * lobe * (half_dot - 1.0) * 20.0 * sigma * (1.0 - sigma),
        jnp.ones(full, jnp.float32),
        jnp.broadcast_to(rim_shape, full),
        jnp.broadcast_to(echo_c[:, None], full),
    ]
    column = gains[:, None]
    resid = observed_c.astype(jnp.float32) - column * shaped
    scaled = [column * piece for piece in jacob]
    surface_normal = []
    for i in range(8):
        for j in range(i, 8):
            surface_normal.append(weight_c * jnp.sum(scaled[i] * scaled[j], axis=0))
    right_side = [weight_c * jnp.sum(piece * resid, axis=0) for piece in scaled]
    lifted = jnp.sum(weight_c * shaped * resid, axis=1)
    energy = jnp.sum(weight_c * shaped * shaped, axis=1)
    return (jnp.stack(surface_normal), jnp.stack(right_side), lifted, energy)


def assemble(observed, weights, params, gains, lights, halves, views, echoes):
    texels = params.shape[1]

    def one_camera(carry, inputs):
        observed_c, weight_c, half_c, view_c, echo_c = inputs
        terms = camera_terms(observed_c, weight_c, params, gains, lights, half_c, view_c, echo_c)
        return (tuple((a + b for a, b in zip(carry, terms))), None)

    start = (
        jnp.zeros((36, texels), jnp.float32),
        jnp.zeros((8, texels), jnp.float32),
        jnp.zeros((LIGHTS,), jnp.float32),
        jnp.zeros((LIGHTS,), jnp.float32),
    )
    result, unused = lax.scan(one_camera, start, (observed, weights, halves, views, echoes))
    return result


def solve_eight(surface_normal, right_side):
    entries = {}
    where = 0
    for i in range(8):
        for j in range(i, 8):
            entries[i, j] = surface_normal[where]
            where += 1
    lower = {}
    for j in range(8):
        accum = entries[j, j] + damping
        for k in range(j):
            accum = accum - lower[j, k] * lower[j, k]
        root = jnp.sqrt(accum)
        lower[j, j] = root
        for i in range(j + 1, 8):
            accum = entries[j, i]
            for k in range(j):
                accum = accum - lower[i, k] * lower[j, k]
            lower[i, j] = accum / root
    forward = []
    for i in range(8):
        accum = right_side[i]
        for k in range(i):
            accum = accum - lower[i, k] * forward[k]
        forward.append(accum / lower[i, i])
    answer = [None] * 8
    for i in range(7, -1, -1):
        accum = forward[i]
        for k in range(i + 1, 8):
            accum = accum - lower[k, i] * answer[k]
        answer[i] = accum / lower[i, i]
    return jnp.stack(answer)


def smooth_tilts(tilt):
    rows = tilt.shape[1]
    cols = tilt.shape[2]
    padded = padded_2(tilt, (("grp", 1), ("tile", 2)), 1)
    boxed = jnp.zeros(tilt.shape, jnp.float32)
    for i in range(3):
        for j in range(3):
            boxed = boxed + padded[:, i : i + rows, j : j + cols]
    return 0.5 * tilt + boxed * (0.5 / 9.0)


def update_gains(gains, lifted, energy):
    totals = lax.psum(jnp.stack([lifted, energy]), ("grp", "tile"))
    return gains + totals[0] / (totals[1] + 1.0)


def on_device(observed, visible, params_start, light_directions, view_dirs, gains_start):
    lights, halves, views, echoes = geometry(light_directions, view_dirs)
    rows = visible.shape[0]
    cols = visible.shape[1]
    shifts = jnp.arange(CAMS, dtype=jnp.int32)
    weights = jnp.bitwise_and(jnp.right_shift(visible.reshape(1, -1), shifts[:, None]), 1).astype(
        jnp.float32
    )
    params = params_start.reshape(8, -1)
    gains = gains_start
    regrouped = lax.all_to_all(observed, "tile", split_axis=2, concat_axis=0, tiled=True)
    flat_obs = regrouped.reshape(CAMS, LIGHTS, rows * cols)
    first_terms = assemble(flat_obs, weights, params, gains, lights, halves, views, echoes)
    for iteration in range(ITERS):
        if iteration == 0:
            surface_normal, right_side, lifted, energy = first_terms
        else:
            surface_normal, right_side, lifted, energy = assemble(
                flat_obs, weights, params, gains, lights, halves, views, echoes
            )
        params = params + solve_eight(surface_normal, right_side)
        gains = update_gains(gains, lifted, energy)
        grid = params.reshape(8, rows, cols)
        params = jnp.concatenate([smooth_tilts(grid[:2]), grid[2:]], axis=0).reshape(8, -1)
    return (params.reshape(8, rows, cols), gains)


def solution(mesh):
    return jax.shard_map(
        on_device,
        mesh=mesh,
        in_specs=(P("tile", "grp", None), P("grp", "tile"), P(None, "grp", "tile"), P(), P(), P()),
        out_specs=(P(None, "grp", "tile"), P()),
        check_vma=False,
    )
```

profile of v0, /device:TPU:3, one launch (start us, length us, event | category | flops | bytes accessed | tf_op | source)
XLA Modules:
  0.0 603.4 jit_solution(8106772559715947173)
XLA Ops:
  0.6 6.7 %copy.16 = bf16[64,8,2048]{0,1,2:T(8,128)(2,1)} copy(bf16[64,8,2048]{2,1,0:T(8,128)(2,1)} %param.12) | data formatting | bytes 4194304 | tf_op args[0]
  7.3 7.6 %reshape.750 = bf16[8,2,65536]{2,1,0:T(2,128)(2,1)} reshape(bf16[2048,8,64]{2,1,0:T(8,128)(2,1)} %bitcast.458) | data formatting | bytes 4194304
  14.9 5.7 all-to-all-start
  22.1 46.7 %all-to-all-done = bf16[8,2,65536]{2,1,0:T(2,128)(2,1)S(1)} async-done(((bf16[8,2,65536]{2,1,0:T(2,128)(2,1)}), bf16[8,2,65536]{2,1,0:T(2,128)(2,1)S(1)}, u32[]{:S(2)}, u32[]{:S(2)}) %all-to-all-start) | async-done | bytes 2097184 | tf_op jit(solution)/shard_map/all_to_all | solution.py:177
  68.8 5.0 reshape.751
  73.8 5.0 copy.17
  78.9 2.4 reshape.745
  81.2 201.9 %while.40 = (s32[]{:T(128)}, f32[36,2048]{1,0:T(8,128)S(1)}, f32[8,2048]{1,0:T(8,128)S(1)}, f32[32]{0:T(128)S(1)}, f32[32]{0:T(128)S(1)}, /*index=5*/f32[16,2048...) while((s32[]{:T(128)}, f32[36,2048]{1,0:T(8,128)S(1)}, ...), condition=%wide.region_51.52_spmd.clone, body=%wide.region_5.51_spmd.clone.sunk | while | flops 14035169 | bytes 4423358 | solution.py:113
  82.5 2.4 multiply_multiply_fusion.36
  95.1 2.4 multiply_multiply_fusion.36
  98.3 1.8 subtract_multiply_fusion.8
  107.8 2.4 multiply_multiply_fusion.36
  120.4 2.4 multiply_multiply_fusion.36
  123.5 1.8 subtract_multiply_fusion.8
  133.0 2.4 multiply_multiply_fusion.36
  145.6 2.4 multiply_multiply_fusion.36
  148.8 1.8 subtract_multiply_fusion.8
  158.2 2.4 multiply_multiply_fusion.36
  170.8 2.4 multiply_multiply_fusion.36
  183.5 2.4 multiply_multiply_fusion.36
  186.6 1.8 subtract_multiply_fusion.8
  196.1 2.4 multiply_multiply_fusion.36
  208.7 2.4 multiply_multiply_fusion.36
  211.8 1.8 subtract_multiply_fusion.8
  221.3 2.4 multiply_multiply_fusion.36
  233.9 2.4 multiply_multiply_fusion.36
  246.5 2.4 multiply_multiply_fusion.36
  259.2 2.4 multiply_multiply_fusion.36
  271.8 2.4 multiply_multiply_fusion.36
  274.9 1.8 subtract_multiply_fusion.8
  284.9 3.1 collective-permute-start
  288.0 2.2 collective-permute-start.1
  290.2 38.6 %psum.14 = f32[2,32]{1,0:T(2,128)S(1)} all-reduce(f32[2,32]{1,0:T(2,128)S(1)} %pad_maximum_fusion.10), channel_id=1, replica_groups=mesh['grp'=4,'tile'=8] {'grp','tile'}, use_global_device_ids=true, to_apply=%region_52.53 | all-reduce | flops 64 | bytes 512 | tf_op jit(solution)/shard_map/psum | solution.py:163
  329.5 5.9 collective-permute-start.2
  335.4 2.1 collective-permute-start.3
  337.5 2.9 collective-permute-done.3
  340.8 203.1 %while.41 = (s32[]{:T(128)}, f32[36,2048]{1,0:T(8,128)S(1)}, f32[8,2048]{1,0:T(8,128)S(1)}, f32[32]{0:T(128)S(1)}, f32[32]{0:T(128)S(1)}, /*index=5*/f32[16,2048...) while((s32[]{:T(128)}, f32[36,2048]{1,0:T(8,128)S(1)}, ...), condition=%wide.region_100.101_spmd.clone, body=%wide.region_54.100_spmd.clone.sunk | while | flops 14035169 | bytes 4423358 | solution.py:113
  342.1 2.4 multiply_multiply_fusion.38
  354.8 2.4 multiply_multiply_fusion.38
  357.9 1.8 subtract_multiply_fusion.9
  367.5 2.4 multiply_multiply_fusion.38
  370.6 1.8 subtract_multiply_fusion.9
  380.2 2.4 multiply_multiply_fusion.38
  383.3 1.8 subtract_multiply_fusion.9
  392.8 2.4 multiply_multiply_fusion.38
  396.0 1.8 subtract_multiply_fusion.9
  405.5 2.4 multiply_multiply_fusion.38
  418.2 2.4 multiply_multiply_fusion.38
  430.9 2.4 multiply_multiply_fusion.38
  443.6 2.4 multiply_multiply_fusion.38
  456.3 2.4 multiply_multiply_fusion.38
  469.0 2.4 multiply_multiply_fusion.38
  481.7 2.4 multiply_multiply_fusion.38
  494.4 2.4 multiply_multiply_fusion.38
  507.1 2.4 multiply_multiply_fusion.38
  519.8 2.4 multiply_multiply_fusion.38
  532.5 2.4 multiply_multiply_fusion.38
  543.9 37.7 %psum.15 = f32[2,32]{1,0:T(2,128)S(1)} all-reduce(f32[2,32]{1,0:T(2,128)S(1)} %pad_maximum_fusion.11), channel_id=1, replica_groups=mesh['grp'=4,'tile'=8] {'grp','tile'}, use_global_device_ids=true, to_apply=%region_101.102 | all-reduce | flops 64 | bytes 512 | tf_op jit(solution)/shard_map/psum | solution.py:163
  583.3 3.1 collective-permute-start.4
  586.4 2.2 collective-permute-start.5
  589.2 2.5 collective-permute-done.5
  591.7 5.8 collective-permute-start.6
  597.6 1.9 collective-permute-start.7
  599.5 3.1 collective-permute-done.7
  (811 shorter events, 311.4 us)
Async XLA Ops:
  14.9 5.8 copy-start.3
  14.9 5.8 copy-start.5
  14.9 6.0 %copy-start.4 = (f32[3,32]{1,0:T(4,128)S(1)}, f32[3,32]{1,0:T(4,128)}, u32[]{:S(2)}) copy-start(f32[3,32]{1,0:T(4,128)} %param.15) | copy-start | bytes 1156
  14.9 6.4 %copy-start.1 = (f32[8,8,256]{2,1,0:T(8,128)S(1)}, f32[8,8,256]{2,1,0:T(8,128)}, u32[]{:S(2)}) copy-start(f32[8,8,256]{2,1,0:T(8,128)} %param.14) | copy-start | bytes 196612
  14.9 6.5 %copy-start.2 = (s32[8,256]{1,0:T(8,128)S(1)}, s32[8,256]{1,0:T(8,128)}, u32[]{:S(2)}) copy-start(s32[8,256]{1,0:T(8,128)} %param.13) | copy-start | bytes 24580
  14.9 6.5 %copy-start = (f32[32]{0:T(128)S(1)}, f32[32]{0:T(128)}, u32[]{:S(2)}) copy-start(f32[32]{0:T(128)} %param.17) | copy-start | bytes 388
  14.9 53.9 %all-to-all-start = ((bf16[8,2,65536]{2,1,0:T(2,128)(2,1)}), bf16[8,2,65536]{2,1,0:T(2,128)(2,1)S(1)}, u32[]{:S(2)}, u32[]{:S(2)}) async-start(bf16[8,2,65536]{2,1,0:T(2,128)(2,1)} %reshape.750), calls=%async_computation | async-start | bytes 4194304 | tf_op jit(solution)/shard_map/all_to_all | solution.py:177
  284.9 44.5 %collective-permute-start = (f32[2,1,256]{2,1,0:T(1,128)S(1)}, f32[2,1,256]{2,1,0:T(1,128)S(1)}, u32[]{:S(2)}, u32[]{:S(2)}) collective-permute-start(f32[2,1,256]{2,1,0:T(1,128)S(1)} %get-tuple-element.1093), channel_id=1, source_target_pairs={{0,8},{8,16},{16,24},{1,9},{9,17},{17,25},{2,10},{10,18},{18,26},{... | collective-permute-start | bytes 6152 | tf_op jit(solution)/shard_map/ppermute | solution.py:21
  288.0 41.4 %collective-permute-start.1 = (f32[2,1,256]{2,1,0:T(1,128)S(1)}, f32[2,1,256]{2,1,0:T(1,128)S(1)}, u32[]{:S(2)}, u32[]{:S(2)}) collective-permute-start(f32[2,1,256]{2,1,0:T(1,128)S(1)} %get-tuple-element.1094), channel_id=1, source_target_pairs={{8,0},{16,8},{24,16},{9,1},{17,9},{25,17},{10,2},{18,10},{26,18},{... | collective-permute-start | bytes 6152 | tf_op jit(solution)/shard_map/ppermute | solution.py:23
  329.5 8.0 %collective-permute-start.2 = (f32[2,10,1]{2,1,0:T(8,128)S(1)}, f32[2,10,1]{2,1,0:T(8,128)S(1)}, u32[]{:S(2)}, u32[]{:S(2)}) collective-permute-start(f32[2,10,1]{2,1,0:T(8,128)S(1)} %get-tuple-element.1081), channel_id=1, source_target_pairs={{0,1},{1,2},{2,3},{3,4},{4,5},{5,6},{6,7},{8,9},{9,10},{10,11},{11... | collective-permute-start | bytes 248 | tf_op jit(solution)/shard_map/ppermute | solution.py:21
  335.4 5.1 collective-permute-start.3
  583.3 5.9 collective-permute-start.4
  586.4 5.2 collective-permute-start.5
  591.7 7.8 %collective-permute-start.6 = (f32[2,10,1]{2,1,0:T(8,128)S(1)}, f32[2,10,1]{2,1,0:T(8,128)S(1)}, u32[]{:S(2)}, u32[]{:S(2)}) collective-permute-start(f32[2,10,1]{2,1,0:T(8,128)S(1)} %get-tuple-element.1079), channel_id=1, source_target_pairs={{0,1},{1,2},{2,3},{3,4},{4,5},{5,6},{6,7},{8,9},{9,10},{10,11},{11... | collective-permute-start | bytes 248 | tf_op jit(solution)/shard_map/ppermute | solution.py:21
  597.6 5.1 collective-permute-start.7
where the time goes:
time: 608 us; the launch traced here: 603 us
  other arithmetic  366 us (60%)
  blocking collectives  76.3 us (13%)
  local copies, waits for them, and re-layouts  67.8 us (11%)
  waiting for transfers between devices  55.2 us (9%)
  starting transfers between devices  32 us (5%)
    mul x32, other arithmetic, camera_terms(): 2.0 * rim_gain * back * view_v  78.1 us
    psum x2, blocking collectives, update_gains(): totals = lax.psum(jnp.stack([lifted, energy]), ('grp', 'tile'))  76.3 us
    reduce_sum x98, other arithmetic, camera_terms(): surface_normal.append(weight_c * jnp.sum(scaled[i] * scaled[j], axis=0))  61.1 us
    mul x32, other arithmetic, camera_terms(): rim_shape = back * back  57.2 us
    all_to_all x1, waiting for transfers between devices, on_device(): lax.all_to_all(observed, 'tile', split_axis=2, concat_axis=0, tiled=True)  46.7 us
    reduce_sum x32, other arithmetic, camera_terms(): lifted = jnp.sum(weight_c * shaped * resid, axis=1)  46.1 us
    mul x32, other arithmetic, camera_terms(): right_side = [weight_c * jnp.sum(piece * resid, axis=0) for piece in scaled]  43.2 us
    reduce_sum x32, other arithmetic, camera_terms(): right_side = [weight_c * jnp.sum(piece * resid, axis=0) for piece in scaled]  41.6 us
  transfers between devices with their start and end apart: 9, of which 4 were waited for; matrix products, arithmetic and copies ran while one was open for 0% of the time, Pallas kernels for 0%

commit v1 on v0

--- a/solution.py
+++ b/solution.py
@@ -160,7 +160,7 @@
 
 
 def update_gains(gains, lifted, energy):
-    totals = lax.psum(jnp.stack([lifted, energy]), ("grp", "tile"))
+    totals = lax.psum(lax.psum(jnp.stack([lifted, energy]), "tile"), "grp")
     return gains + totals[0] / (totals[1] + 1.0)
 
 

time: 608 us -> 567 us (0.933)
  blocking collectives: 76.3 us -> 41 us
    psum x2 -> x4, blocking collectives: 76.3 us -> 41 us  [update_gains(): totals = lax.psum(lax.psum(jnp.stack([lifted, energy]), 'tile'), 'grp')]
where the time goes in v1:
time: 567 us; the launch traced here: 563 us
  other arithmetic  366 us (65%)
  local copies, waits for them, and re-layouts  67.8 us (12%)
  waiting for transfers between devices  51.7 us (9%)
  blocking collectives  41 us (7%)
  starting transfers between devices  30.6 us (5%)
    mul x32, other arithmetic, camera_terms(): 2.0 * rim_gain * back * view_v  78.1 us
    reduce_sum x98, other arithmetic, camera_terms(): surface_normal.append(weight_c * jnp.sum(scaled[i] * scaled[j], axis=0))  61 us
    mul x32, other arithmetic, camera_terms(): rim_shape = back * back  57.2 us
    all_to_all x1, waiting for transfers between devices, on_device(): lax.all_to_all(observed, 'tile', split_axis=2, concat_axis=0, tiled=True)  46.7 us
    reduce_sum x32, other arithmetic, camera_terms(): lifted = jnp.sum(weight_c * shaped * resid, axis=1)  46.1 us
    mul x32, other arithmetic, camera_terms(): right_side = [weight_c * jnp.sum(piece * resid, axis=0) for piece in scaled]  43.2 us
    reduce_sum x32, other arithmetic, camera_terms(): right_side = [weight_c * jnp.sum(piece * resid, axis=0) for piece in scaled]  41.8 us
    psum x4, blocking collectives, update_gains(): totals = lax.psum(lax.psum(jnp.stack([lifted, energy]), 'tile'), 'grp')  41 us
  transfers between devices with their start and end apart: 9, of which 4 were waited for; matrix products, arithmetic and copies ran while one was open for 0% of the time, Pallas kernels for 0%

profile of v1, /device:TPU:3, one launch (start us, length us, event | category | flops | bytes accessed | tf_op | source)
XLA Modules:
  0.0 563.3 jit_solution(9645166580960655963)
XLA Ops:
  0.6 6.7 %copy.16 = bf16[64,8,2048]{0,1,2:T(8,128)(2,1)} copy(bf16[64,8,2048]{2,1,0:T(8,128)(2,1)} %param.12) | data formatting | bytes 4194304 | tf_op args[0]
  7.3 7.6 %reshape.750 = bf16[8,2,65536]{2,1,0:T(2,128)(2,1)} reshape(bf16[2048,8,64]{2,1,0:T(8,128)(2,1)} %bitcast.458) | data formatting | bytes 4194304
  14.9 5.7 %all-to-all-start = ((bf16[8,2,65536]{2,1,0:T(2,128)(2,1)}), bf16[8,2,65536]{2,1,0:T(2,128)(2,1)S(1)}, u32[]{:S(2)}, u32[]{:S(2)}) async-start(bf16[8,2,65536]{2,1,0:T(2,128)(2,1)} %reshape.750), calls=%async_computation | async-start | bytes 4194304 | tf_op jit(solution)/shard_map/all_to_all | solution.py:177
  22.1 46.7 %all-to-all-done = bf16[8,2,65536]{2,1,0:T(2,128)(2,1)S(1)} async-done(((bf16[8,2,65536]{2,1,0:T(2,128)(2,1)}), bf16[8,2,65536]{2,1,0:T(2,128)(2,1)S(1)}, u32[]{:S(2)}, u32[]{:S(2)}) %all-to-all-start) | async-done | bytes 2097184 | tf_op jit(solution)/shard_map/all_to_all | solution.py:177
  68.8 5.0 reshape.751
  73.8 5.0 copy.17
  78.9 2.4 reshape.745
  81.2 201.9 %while.40 = (s32[]{:T(128)}, f32[36,2048]{1,0:T(8,128)S(1)}, f32[8,2048]{1,0:T(8,128)S(1)}, f32[32]{0:T(128)S(1)}, f32[32]{0:T(128)S(1)}, /*index=5*/f32[16,2048...) while((s32[]{:T(128)}, f32[36,2048]{1,0:T(8,128)S(1)}, ...), condition=%wide.region_51.52_spmd.clone, body=%wide.region_5.51_spmd.clone.sunk | while | flops 14035169 | bytes 4423358 | solution.py:113
  82.5 2.4 multiply_multiply_fusion.36
  95.1 2.4 multiply_multiply_fusion.36
  98.3 1.8 subtract_multiply_fusion.8
  107.8 2.4 multiply_multiply_fusion.36
  120.4 2.4 multiply_multiply_fusion.36
  123.5 1.8 subtract_multiply_fusion.8
  133.0 2.4 multiply_multiply_fusion.36
  145.6 2.4 multiply_multiply_fusion.36
  158.2 2.4 multiply_multiply_fusion.36
  161.4 1.8 subtract_multiply_fusion.8
  170.9 2.4 multiply_multiply_fusion.36
  183.5 2.4 multiply_multiply_fusion.36
  196.1 2.4 multiply_multiply_fusion.36
  199.2 1.8 subtract_multiply_fusion.8
  208.7 2.4 multiply_multiply_fusion.36
  221.3 2.4 multiply_multiply_fusion.36
  233.9 2.4 multiply_multiply_fusion.36
  237.1 1.8 subtract_multiply_fusion.8
  246.6 2.4 multiply_multiply_fusion.36
  259.2 2.4 multiply_multiply_fusion.36
  262.3 1.8 subtract_multiply_fusion.8
  271.8 2.4 multiply_multiply_fusion.36
  284.9 3.1 collective-permute-start
  288.0 2.2 collective-permute-start.1
  290.2 14.4 %psum.28 = f32[2,32]{1,0:T(2,128)S(1)} all-reduce(f32[2,32]{1,0:T(2,128)S(1)} %pad_maximum_fusion.10), channel_id=1, replica_groups=mesh['grp'=4,'tile'=8] {'tile'}, use_global_device_ids=true, to_apply=%region_52.53 | all-reduce | flops 64 | bytes 512 | tf_op jit(solution)/shard_map/psum | solution.py:163
  304.6 6.9 %psum.29 = f32[2,32]{1,0:T(2,128)S(1)} all-reduce(f32[2,32]{1,0:T(2,128)S(1)} %psum.28), channel_id=1, replica_groups=mesh['grp'=4,'tile'=8] {'grp'}, use_global_device_ids=true, to_apply=%region_53.54 | all-reduce | flops 64 | bytes 512 | tf_op jit(solution)/shard_map/psum | solution.py:163
  312.3 2.5 collective-permute-start.2
  314.8 3.9 collective-permute-start.3
  320.1 203.2 %while.41 = (s32[]{:T(128)}, f32[36,2048]{1,0:T(8,128)S(1)}, f32[8,2048]{1,0:T(8,128)S(1)}, f32[32]{0:T(128)S(1)}, f32[32]{0:T(128)S(1)}, /*index=5*/f32[16,2048...) while((s32[]{:T(128)}, f32[36,2048]{1,0:T(8,128)S(1)}, ...), condition=%wide.region_101.102_spmd.clone, body=%wide.region_55.101_spmd.clone.sunk | while | flops 14035169 | bytes 4423358 | solution.py:113
  321.4 2.4 multiply_multiply_fusion.38
  334.1 2.4 multiply_multiply_fusion.38
  337.3 1.8 subtract_multiply_fusion.9
  346.8 2.4 multiply_multiply_fusion.38
  359.5 2.4 multiply_multiply_fusion.38
  372.2 2.4 multiply_multiply_fusion.38
  375.4 1.8 subtract_multiply_fusion.9
  384.9 2.4 multiply_multiply_fusion.38
  397.6 2.4 multiply_multiply_fusion.38
  410.3 2.4 multiply_multiply_fusion.38
  413.5 1.8 subtract_multiply_fusion.9
  423.0 2.4 multiply_multiply_fusion.38
  435.7 2.4 multiply_multiply_fusion.38
  438.9 1.8 subtract_multiply_fusion.9
  448.4 2.4 multiply_multiply_fusion.38
  461.1 2.4 multiply_multiply_fusion.38
  473.8 2.4 multiply_multiply_fusion.38
  486.5 2.4 multiply_multiply_fusion.38
  499.2 2.4 multiply_multiply_fusion.38
  511.9 2.4 multiply_multiply_fusion.38
  523.3 12.8 %psum.30 = f32[2,32]{1,0:T(2,128)S(1)} all-reduce(f32[2,32]{1,0:T(2,128)S(1)} %pad_maximum_fusion.11), channel_id=1, replica_groups=mesh['grp'=4,'tile'=8] {'tile'}, use_global_device_ids=true, to_apply=%region_102.103 | all-reduce | flops 64 | bytes 512 | tf_op jit(solution)/shard_map/psum | solution.py:163
  536.1 6.9 %psum.31 = f32[2,32]{1,0:T(2,128)S(1)} all-reduce(f32[2,32]{1,0:T(2,128)S(1)} %psum.30), channel_id=1, replica_groups=mesh['grp'=4,'tile'=8] {'grp'}, use_global_device_ids=true, to_apply=%region_103.104 | all-reduce | flops 64 | bytes 512 | tf_op jit(solution)/shard_map/psum | solution.py:163
  544.7 3.1 collective-permute-start.4
  547.8 2.2 collective-permute-start.5
  550.6 2.5 collective-permute-done.5
  553.2 4.3 collective-permute-start.6
  557.5 3.7 collective-permute-start.7
  (813 shorter events, 314.1 us)
Async XLA Ops:
  14.9 5.8 %copy-start.3 = (f32[3,16]{1,0:T(4,128)S(1)}, f32[3,16]{1,0:T(4,128)}, u32[]{:S(2)}) copy-start(f32[3,16]{1,0:T(4,128)} %param.16) | copy-start | bytes 580
  14.9 5.8 %copy-start.5 = (f32[3]{0:T(128)S(1)}, f32[3]{0:T(128)}, u32[]{:S(2)}) copy-start(f32[3]{0:T(128)} %constant.128.clone) | copy-start | bytes 40
  14.9 6.0 %copy-start.4 = (f32[3,32]{1,0:T(4,128)S(1)}, f32[3,32]{1,0:T(4,128)}, u32[]{:S(2)}) copy-start(f32[3,32]{1,0:T(4,128)} %param.15) | copy-start | bytes 1156
  14.9 6.4 %copy-start.1 = (f32[8,8,256]{2,1,0:T(8,128)S(1)}, f32[8,8,256]{2,1,0:T(8,128)}, u32[]{:S(2)}) copy-start(f32[8,8,256]{2,1,0:T(8,128)} %param.14) | copy-start | bytes 196612
  14.9 6.5 %copy-start.2 = (s32[8,256]{1,0:T(8,128)S(1)}, s32[8,256]{1,0:T(8,128)}, u32[]{:S(2)}) copy-start(s32[8,256]{1,0:T(8,128)} %param.13) | copy-start | bytes 24580
  14.9 6.5 %copy-start = (f32[32]{0:T(128)S(1)}, f32[32]{0:T(128)}, u32[]{:S(2)}) copy-start(f32[32]{0:T(128)} %param.17) | copy-start | bytes 388
  14.9 53.9 %all-to-all-start = ((bf16[8,2,65536]{2,1,0:T(2,128)(2,1)}), bf16[8,2,65536]{2,1,0:T(2,128)(2,1)S(1)}, u32[]{:S(2)}, u32[]{:S(2)}) async-start(bf16[8,2,65536]{2,1,0:T(2,128)(2,1)} %reshape.750), calls=%async_computation | async-start | bytes 4194304 | tf_op jit(solution)/shard_map/all_to_all | solution.py:177
  284.9 27.2 %collective-permute-start = (f32[2,1,256]{2,1,0:T(1,128)S(1)}, f32[2,1,256]{2,1,0:T(1,128)S(1)}, u32[]{:S(2)}, u32[]{:S(2)}) collective-permute-start(f32[2,1,256]{2,1,0:T(1,128)S(1)} %get-tuple-element.1093), channel_id=1, source_target_pairs={{0,8},{8,16},{16,24},{1,9},{9,17},{17,25},{2,10},{10,18},{18,26},{... | collective-permute-start | bytes 6152 | tf_op jit(solution)/shard_map/ppermute | solution.py:21
  288.0 24.1 %collective-permute-start.1 = (f32[2,1,256]{2,1,0:T(1,128)S(1)}, f32[2,1,256]{2,1,0:T(1,128)S(1)}, u32[]{:S(2)}, u32[]{:S(2)}) collective-permute-start(f32[2,1,256]{2,1,0:T(1,128)S(1)} %get-tuple-element.1094), channel_id=1, source_target_pairs={{8,0},{16,8},{24,16},{9,1},{17,9},{25,17},{10,2},{18,10},{26,18},{... | collective-permute-start | bytes 6152 | tf_op jit(solution)/shard_map/ppermute | solution.py:23
  312.3 6.4 %collective-permute-start.2 = (f32[2,10,1]{2,1,0:T(8,128)S(1)}, f32[2,10,1]{2,1,0:T(8,128)S(1)}, u32[]{:S(2)}, u32[]{:S(2)}) collective-permute-start(f32[2,10,1]{2,1,0:T(8,128)S(1)} %get-tuple-element.1081), channel_id=1, source_target_pairs={{0,1},{1,2},{2,3},{3,4},{4,5},{5,6},{6,7},{8,9},{9,10},{10,11},{11... | collective-permute-start | bytes 248 | tf_op jit(solution)/shard_map/ppermute | solution.py:21
  314.8 5.1 collective-permute-start.3
  544.7 5.9 %collective-permute-start.4 = (f32[2,1,256]{2,1,0:T(1,128)S(1)}, f32[2,1,256]{2,1,0:T(1,128)S(1)}, u32[]{:S(2)}, u32[]{:S(2)}) collective-permute-start(f32[2,1,256]{2,1,0:T(1,128)S(1)} %get-tuple-element.1087), channel_id=1, source_target_pairs={{0,8},{8,16},{16,24},{1,9},{9,17},{17,25},{2,10},{10,18},{18,26},{... | collective-permute-start | bytes 6152 | tf_op jit(solution)/shard_map/ppermute | solution.py:21
  547.8 5.2 collective-permute-start.5
  553.2 8.0 %collective-permute-start.6 = (f32[2,10,1]{2,1,0:T(8,128)S(1)}, f32[2,10,1]{2,1,0:T(8,128)S(1)}, u32[]{:S(2)}, u32[]{:S(2)}) collective-permute-start(f32[2,10,1]{2,1,0:T(8,128)S(1)} %get-tuple-element.1079), channel_id=1, source_target_pairs={{0,1},{1,2},{2,3},{3,4},{4,5},{5,6},{6,7},{8,9},{9,10},{10,11},{11... | collective-permute-start | bytes 248 | tf_op jit(solution)/shard_map/ppermute | solution.py:21
  557.5 5.1 collective-permute-start.7
